TPU v7x, 128 devices: a whole 4x4x4 slice. The times are simulated.
128 devices in a mesh: col: 32 (over x, z, core), leg: 4 (over y).
Axes of the slice: x: 4, y: 4, z: 4, core: 2. Of those that a mesh axis runs over, the one named last changes fastest.
Arguments:
- coeffs: float32 [2048, 4, 128, 128], P(('col', 'leg')), may hold values from -0.5 to 0.5
- block_ids: int32 [2048, 4], P(('col', 'leg')), may hold values from 0 to 127
- col_counts: int32 [2048], P(('col', 'leg')), may hold values from 1 to 128
- primal: float32 [2048, 128], P(('col', 'leg')), may hold values from 0.3 to 3
- slack: float32 [2048, 128], P(('col', 'leg')), may hold values from 0.3 to 3
- cost: float32 [2048, 128], P(('col', 'leg')), may hold values from -6 to 6
- duals: float32 [128, 128], P('leg'), may hold values from -6 to 6
- demand: float32 [128, 128], P('leg'), may hold values from -6 to 6
Outputs:
- step_dual: float32 [128, 128], P('leg')
- step_primal: float32 [2048, 128], P(('col', 'leg'))
Inputs may be any that keep to these rules, and one draw needn't show every extreme that they name: `block_ids`: leg block of each tile; many tiles may share a block, the tiles of one column group too. `col_counts`: columns at or after this count in a column group are padding.
All inputs are finite; a program needn't handle non-finite values.
Results may differ from a plain program's by a relative error of at most 0.0003.
Values sent between devices are 32-bit elements; how exact they have to be, the bound alone decides.
No kernel may reach another device: no remote copies, remote signals or barrier semaphores. Data moves between devices by JAX's collectives and lax.ppermute only.
A program may use at most 128 MiB of HBM per device.

v0:
```python
import jax
import jax.numpy as jnp
from jax import lax
from jax.sharding import PartitionSpec as P

ITERS = 3
SIGMA = 0.3
REGULAR = 1.0
PRECISE = lax.Precision.HIGHEST


def invert_blocks(blocks):
    identity = jnp.eye(blocks.shape[1], dtype=jnp.float32)

    def invert_one(matrix):
        factor = jnp.linalg.cholesky(matrix)
        return jax.scipy.linalg.cho_solve((factor, True), identity)

    return jax.vmap(invert_one)(blocks + REGULAR * identity)


def per_device(coeffs, block_ids, col_counts, primal, slack, cost, duals, demand):
    lb_dev = duals.shape[0]
    group_count = coeffs.shape[0]
    span = coeffs.shape[1]
    rows_tile = coeffs.shape[2]
    columns = coeffs.shape[3]
    tile_count = group_count * span
    leg_count = lax.axis_size("leg")
    total_blocks = lb_dev * leg_count
    valid = (jnp.arange(columns, dtype=jnp.int32)[None, :] < col_counts[:, None]).astype(
        jnp.float32
    )
    tile_vals = coeffs * valid[:, None, None, :]
    totals_pair = lax.psum((jnp.sum(valid * primal * slack), jnp.sum(valid)), ("col", "leg"))
    mean_comp = totals_pair[0] / totals_pair[1]
    scaling = primal / slack
    flat_ids = block_ids.reshape(tile_count)
    all_duals = lax.all_gather(duals, "leg", axis=0, tiled=True)
    natural_hot = (flat_ids[:, None] == jnp.arange(total_blocks, dtype=jnp.int32)[None, :]).astype(
        jnp.float32
    )
    dual_tiles = jnp.dot(natural_hot, all_duals, precision=PRECISE).reshape(
        group_count, span, rows_tile
    )
    dual_res = cost - jnp.einsum("gsij,gsi->gj", tile_vals, dual_tiles, precision=PRECISE) - slack
    comp_res = SIGMA * mean_comp - primal * slack
    shifted = primal - scaling * dual_res + comp_res / slack

    def widen_all(vector):
        return lax.all_gather(vector, "leg", axis=0, tiled=True)

    def inner_sum(left, right):
        return lax.psum(jnp.sum(left * right), "leg")

    onehot = (flat_ids[:, None] == jnp.arange(total_blocks, dtype=jnp.int32)[None, :]).astype(
        jnp.float32
    )

    def transpose_apply(whole):
        per_tile = jnp.dot(onehot, whole, precision=PRECISE).reshape(group_count, span, rows_tile)
        return jnp.einsum("gsij,gsi->gj", tile_vals, per_tile, precision=PRECISE)

    def forward_partial(colvec):
        per_tile = jnp.einsum("gsij,gj->gsi", tile_vals, colvec, precision=PRECISE)
        return jnp.dot(onehot.T, per_tile.reshape(tile_count, rows_tile), precision=PRECISE)

    rhs_part = -forward_partial(shifted)
    weighted = tile_vals * scaling[:, None, None, :]
    gram = jnp.einsum("gsij,gskj->gsik", weighted, tile_vals, precision=PRECISE)
    gram = gram.reshape(tile_count, rows_tile, rows_tile)
    block_part = jnp.einsum("tb,tik->bik", onehot, gram, precision=PRECISE)
    rhs_sum, block_sum = lax.psum(
        (
            lax.psum_scatter(rhs_part, "leg", scatter_dimension=0, tiled=True),
            lax.psum_scatter(block_part, "leg", scatter_dimension=0, tiled=True),
        ),
        "col",
    )
    rhs = demand + rhs_sum
    inverse = invert_blocks(block_sum)

    def precondition(vector):
        return jnp.einsum("bij,bj->bi", inverse, vector, precision=PRECISE)

    step_dual = jnp.zeros_like(rhs)
    residual = rhs
    smoothed = precondition(residual)
    direction = smoothed
    norm_now = inner_sum(residual, smoothed)
    for turn in range(ITERS):
        operate_whole = widen_all(direction)
        narrow_shares = lax.psum_scatter(
            forward_partial(scaling * transpose_apply(operate_whole)),
            "leg",
            scatter_dimension=0,
            tiled=True,
        )
        image = lax.psum(narrow_shares, "col") + REGULAR * direction
        step_len = norm_now / inner_sum(direction, image)
        step_dual = step_dual + step_len * direction
        residual = residual - step_len * image
        if turn + 1 < ITERS:
            smoothed = precondition(residual)
            norm_next = inner_sum(residual, smoothed)
            direction = smoothed + norm_next / norm_now * direction
            norm_now = norm_next
    whole_step = widen_all(step_dual)
    step_primal = valid * (
        scaling * transpose_apply(whole_step) + comp_res / slack - scaling * dual_res
    )
    return (
        lax.dynamic_slice_in_dim(whole_step, lax.axis_index("leg") * lb_dev, lb_dev, 0),
        step_primal,
    )


def solution(mesh):
    return jax.shard_map(
        per_device,
        mesh=mesh,
        in_specs=(
            P(("col", "leg"), None, None, None),
            P(("col", "leg"), None),
            P(("col", "leg")),
            P(("col", "leg"), None),
            P(("col", "leg"), None),
            P(("col", "leg"), None),
            P("leg", None),
            P("leg", None),
        ),
        out_specs=(P("leg", None), P(("col", "leg"), None)),
        check_vma=False,
    )
```

profile of v0, /device:TPU:0, one launch (start us, length us, event | category | flops | bytes accessed | tf_op | source)
XLA Modules:
  0.0 1638.2 jit_solution(10132136737136496447)
XLA Ops:
  8.1 12.7 all_gather.15
  21.7 1.4 fusion.43
  23.1 66.0 %all-reduce = (f32[]{:T(128)}, f32[]{:T(128)}) all-reduce(f32[]{:T(128)} %get-tuple-element.5, f32[]{:T(128)} %get-tuple-element.4), channel_id=1, replica_groups=mesh['col'=32,'leg'=4] {'col','leg'}, use_global_device_ids=true, to_apply=%region_1.0 | all-reduce | flops 2 | bytes 16 | tf_op jit(solution)/shard_map/psum | solution.py:35
  90.5 4.3 fusion.18
  94.9 8.9 fusion
  103.8 9.5 fusion.2
  113.3 9.3 copy.22
  122.7 5.9 fusion.17
  128.6 1.0 convolution_negate_fusion
  129.6 71.0 %reduce-scatter.8.cloned.1.call-done = f32[32,128,128]{1,2,0:T(8,128)} async-done(((f32[128,128,128]{1,2,0:T(8,128)}), f32[32,128,128]{1,2,0:T(8,128)}) %reduce-scatter.8.cloned.1.call-update) | async-done | bytes 2097168 | tf_op jit(solution)/shard_map/reduce_scatter | solution.py:76
  200.8 22.1 %reduce-scatter.6.cloned.1.call-done = f32[32,128]{1,0:T(8,128)} async-done(((f32[128,128]{1,0:T(8,128)}), f32[32,128]{1,0:T(8,128)}) %reduce-scatter.6.cloned.1.call-update) | async-done | bytes 16400 | tf_op jit(solution)/shard_map/reduce_scatter | solution.py:75
  223.0 126.4 %psum.93 = f32[32,128]{1,0:T(8,128)S(1)} all-reduce(f32[32,128]{1,0:T(8,128)} %reduce-scatter.6.cloned.1.call-done), channel_id=1, replica_groups=mesh['col'=32,'leg'=4] {'col'}, use_global_device_ids=true, to_apply=%region_5.0 | all-reduce | flops 4096 | bytes 32768 | tf_op jit(solution)/shard_map/psum | solution.py:73
  349.4 3.3 broadcast_add_fusion
  352.7 2.9 copy.24
  355.6 3.2 fusion.8
  358.9 375.8 %custom-call.11 = f32[32,128,128]{2,1,0:T(8,128)S(1)} custom-call(f32[32,128,128]{2,1,0:T(8,128)} %fusion.8), custom_call_target="Cholesky" | custom-call | tf_op jit(solution)/shard_map/vmap(jit(cholesky))/cholesky | solution.py:16
  734.9 1.7 select_bitcast_fusion
  736.6 315.3 %custom-call.12 = f32[32,1,128,128]{2,3,1,0:T(8,128)S(1)} custom-call(f32[32,1,128,128]{3,2,1,0:T(8,128)} %select_bitcast_fusion), custom_call_target="InvertDiagBlocksLowerTriangular" | custom-call | tf_op jit(solution)/shard_map/vmap(jit(_cho_solve))/triangular_solve | solution.py:17
  1051.9 1.3 copy-done.5
  1053.2 3.5 fusion.6
  1056.8 4.0 fusion.4
  1060.7 3.3 fusion.44
  1064.1 12.3 all_gather.16
  1076.6 2.5 fusion.15
  1079.1 3.7 fusion.14
  1083.8 15.1 reduce-scatter.10.cloned.1.call-done
  1099.0 126.0 %psum.96 = f32[32,128]{1,0:T(8,128)S(1)} all-reduce(f32[32,128]{1,0:T(8,128)} %reduce-scatter.10.cloned.1.call-done), channel_id=1, replica_groups=mesh['col'=32,'leg'=4] {'col'}, use_global_device_ids=true, to_apply=%region_13.14 | all-reduce | flops 4096 | bytes 32768 | tf_op jit(solution)/shard_map/psum | solution.py:99
  1225.6 9.7 all-reduce.1
  1236.6 3.3 fusion.45
  1240.6 9.0 psum.98
  1250.9 12.2 all_gather.17
  1263.3 4.2 fusion.13
  1267.5 3.7 fusion.12
  1271.3 1.0 fusion.23
  1272.3 15.1 reduce-scatter.12.cloned.1.call-done
  1287.4 126.0 %psum.99 = f32[32,128]{1,0:T(8,128)S(1)} all-reduce(f32[32,128]{1,0:T(8,128)} %reduce-scatter.12.cloned.1.call-done), channel_id=1, replica_groups=mesh['col'=32,'leg'=4] {'col'}, use_global_device_ids=true, to_apply=%region_19.20 | all-reduce | flops 4096 | bytes 32768 | tf_op jit(solution)/shard_map/psum | solution.py:99
  1414.0 9.7 psum.100
  1425.1 3.3 fusion.46
  1429.1 9.0 psum.101
  1439.4 12.2 all_gather.18
  1451.8 4.2 fusion.11
  1456.0 3.7 fusion.10
  1459.8 1.0 fusion.21
  1460.7 15.2 reduce-scatter.14.cloned.1.call-done
  1475.9 126.0 %psum.102 = f32[32,128]{1,0:T(8,128)S(1)} all-reduce(f32[32,128]{1,0:T(8,128)} %reduce-scatter.14.cloned.1.call-done), channel_id=1, replica_groups=mesh['col'=32,'leg'=4] {'col'}, use_global_device_ids=true, to_apply=%region_25.26 | all-reduce | flops 4096 | bytes 32768 | tf_op jit(solution)/shard_map/psum | solution.py:99
  1602.5 9.7 psum.103
  1613.6 11.9 all_gather.19
  1625.7 4.2 fusion.16
  (66 shorter events, 8.9 us)
Async XLA Ops:
  7.2 87.7 %copy-start.6 = (f32[16,128]{1,0:T(8,128)S(1)}, f32[16,128]{1,0:T(8,128)}, u32[]{:S(2)}) copy-start(f32[16,128]{1,0:T(8,128)} %param.11) | copy-start | bytes 24580
  7.2 87.7 %copy-start.7 = (f32[16,128]{1,0:T(8,128)S(1)}, f32[16,128]{1,0:T(8,128)}, u32[]{:S(2)}) copy-start(f32[16,128]{1,0:T(8,128)} %param.12) | copy-start | bytes 24580
  7.2 87.7 %copy-start.8 = (f32[16,128]{1,0:T(8,128)S(1)}, f32[16,128]{1,0:T(8,128)}, u32[]{:S(2)}) copy-start(f32[16,128]{1,0:T(8,128)} %param.13) | copy-start | bytes 24580
  7.2 193.4 %reduce-scatter.8.cloned.1.call-start = ((), (), s32[]{:S(2)}) async-start(), calls=%async_computation.6 | async-start | bytes 10485760 | tf_op jit(solution)/shard_map/reduce_scatter | solution.py:76
  90.5 4.4 copy-start
  122.6 226.7 %copy-start.9 = (f32[32,128]{1,0:T(8,128)S(1)}, f32[32,128]{1,0:T(8,128)}, u32[]{:S(2)}) copy-start(f32[32,128]{1,0:T(8,128)} %param.15) | copy-start | bytes 49156
  122.7 100.3 %reduce-scatter.6.cloned.1.call-start = ((), (), s32[]{:S(2)}) async-start(), calls=%async_computation.5 | async-start | bytes 81920 | tf_op jit(solution)/shard_map/reduce_scatter | solution.py:75
  129.6 219.8 %all-reduce.4.cloned.1.call-start = ((), (), s32[]{:S(2)}) async-start(), calls=%async_computation.7 | async-start | bytes 4194304 | tf_op jit(solution)/shard_map/psum | solution.py:73
  200.6 898.3 %reduce-scatter.10.cloned.1.call-start = ((), (), s32[]{:S(2)}) async-start(), calls=%async_computation.8 | async-start | bytes 81920 | tf_op jit(solution)/shard_map/reduce_scatter | solution.py:93
  349.4 6.2 copy-start.4
  1051.9 1.4 copy-start.5
  1056.7 19.9 %copy-start.1 = (f32[16,4,128,128]{3,2,1,0:T(8,128)S(1)}, f32[16,4,128,128]{3,2,1,0:T(8,128)}, u32[]{:S(2)}) copy-start(f32[16,4,128,128]{3,2,1,0:T(8,128)} %param.8) | copy-start | bytes 12582916
  1083.8 203.6 %reduce-scatter.12.cloned.1.call-start = ((), (), s32[]{:S(2)}) async-start(), calls=%async_computation.9 | async-start | bytes 81920 | tf_op jit(solution)/shard_map/reduce_scatter | solution.py:93
  1250.9 16.6 %copy-start.2 = (f32[16,4,128,128]{3,2,1,0:T(8,128)S(1)}, f32[16,4,128,128]{3,2,1,0:T(8,128)}, u32[]{:S(2)}) copy-start(f32[16,4,128,128]{3,2,1,0:T(8,128)} %param.8) | copy-start | bytes 12582916
  1272.2 203.7 %reduce-scatter.14.cloned.1.call-start = ((), (), s32[]{:S(2)}) async-start(), calls=%async_computation.10 | async-start | bytes 81920 | tf_op jit(solution)/shard_map/reduce_scatter | solution.py:93
  1439.4 16.7 %copy-start.3 = (f32[16,4,128,128]{3,2,1,0:T(8,128)S(1)}, f32[16,4,128,128]{3,2,1,0:T(8,128)}, u32[]{:S(2)}) copy-start(f32[16,4,128,128]{3,2,1,0:T(8,128)} %param.8) | copy-start | bytes 12582916
  1456.0 173.8 %copy-start.10 = (s32[16]{0:T(128)S(1)}, s32[16]{0:T(128)}, u32[]{:S(2)}) copy-start(s32[16]{0:T(128)} %param.10) | copy-start | bytes 196
Sparse Core Ops, SparseCore 0:
  122.8 77.7 reduce-scatter.7
  202.9 19.9 reduce-scatter.5
  226.6 107.2 all-reduce.3
  1083.9 15.0 reduce-scatter.9
  1272.4 14.9 reduce-scatter.11
  1460.9 15.0 reduce-scatter.13
where the time goes:
time: 1650 us; the launch traced here: 1640 us
  other arithmetic  706 us (43%)
  blocking collectives  679 us (41%)
  waiting for transfers between devices  139 us (8%)
  matrix products  77.1 us (5%)
  between operations  22.8 us (1%)
    psum x3, blocking collectives, per_device(): image = lax.psum(narrow_shares, 'col') + REGULAR * direction  378 us
    another operation x4, other arithmetic, invert_one(): factor = jnp.linalg.cholesky(matrix)  376 us
    another operation x3, other arithmetic, invert_one(): return jax.scipy.linalg.cho_solve((factor, True), identity)  317 us
    psum x1, blocking collectives, per_device(): lax.psum((lax.psum_scatter(rhs_part, 'leg', scatter_dimension=0, tiled=Tr...  126 us
    reduce_scatter x1, waiting for transfers between devices, per_device(): lax.psum_scatter(block_part, 'leg', scatter_dimension=0, tiled=True)  71 us
    psum x1, blocking collectives, per_device(): lax.psum((jnp.sum(valid * primal * slack), jnp.sum(valid)), ('col', 'leg'))  66 us
    all_gather x4, blocking collectives, widen_all(): return lax.all_gather(vector, 'leg', axis=0, tiled=True)  48.6 us
    psum x5, blocking collectives, inner_sum(): return lax.psum(jnp.sum(left * right), 'leg')  47.1 us
  transfers between devices with their start and end apart: 6, of which 5 were waited for; matrix products, arithmetic and copies ran while one was open for 0% of the time, Pallas kernels for 0%

commit v1 on v0

--- a/solution.py
+++ b/solution.py
@@ -96,7 +96,7 @@
             scatter_dimension=0,
             tiled=True,
         )
-        image = lax.psum(narrow_shares, "col") + REGULAR * direction
+        image = jnp.sum(lax.all_gather(narrow_shares, "col"), axis=0) + REGULAR * direction
         step_len = norm_now / inner_sum(direction, image)
         step_dual = step_dual + step_len * direction
         residual = residual - step_len * image

time: 1650 us -> 1350 us (0.82)
  blocking collectives: 679 us -> 375 us
    psum x3 -> x0, blocking collectives: 378 us -> none  [per_device(): image = lax.psum(narrow_shares, 'col') + REGULAR * direction]
    all_gather x0 -> x3, blocking collectives: none -> 74.8 us  [per_device(): lax.all_gather(narrow_shares, 'col')]
  transfers between devices with their start and end apart: 6 -> 6, of which waited for: 5 -> 5; matrix products, arithmetic and copies ran while one was open for 0% -> 1% of each run, Pallas kernels for 0% -> 0%
where the time goes in v1:
time: 1350 us; the launch traced here: 1340 us
  other arithmetic  706 us (52%)
  blocking collectives  375 us (28%)
  waiting for transfers between devices  145 us (11%)
  matrix products  77.1 us (6%)
  between operations  23 us (2%)
  local copies, waits for them, and re-layouts  15.2 us (1%)
    another operation x4, other arithmetic, invert_one(): factor = jnp.linalg.cholesky(matrix)  376 us
    another operation x3, other arithmetic, invert_one(): return jax.scipy.linalg.cho_solve((factor, True), identity)  317 us
    psum x1, blocking collectives, per_device(): lax.psum((lax.psum_scatter(rhs_part, 'leg', scatter_dimension=0, tiled=Tr...  126 us
    all_gather x3, blocking collectives, per_device(): lax.all_gather(narrow_shares, 'col')  74.8 us
    reduce_scatter x1, waiting for transfers between devices, per_device(): lax.psum_scatter(block_part, 'leg', scatter_dimension=0, tiled=True)  71 us
    psum x1, blocking collectives, per_device(): lax.psum((jnp.sum(valid * primal * slack), jnp.sum(valid)), ('col', 'leg'))  66 us
    reduce_scatter x3, waiting for transfers between devices, per_device(): lax.psum_scatter(forward_partial(scaling * transpose_apply(operate_whole)...  51.4 us
    all_gather x4, blocking collectives, widen_all(): return lax.all_gather(vector, 'leg', axis=0, tiled=True)  48.4 us
  transfers between devices with their start and end apart: 6, of which 5 were waited for; matrix products, arithmetic and copies ran while one was open for 1% of the time, Pallas kernels for 0%

profile of v1, /device:TPU:0, one launch (start us, length us, event | category | flops | bytes accessed | tf_op | source)
XLA Modules:
  0.0 1340.9 jit_solution(6864509317757547336)
XLA Ops:
  8.1 12.7 all_gather.33
  21.7 1.4 fusion.43
  23.1 66.0 %all-reduce = (f32[]{:T(128)}, f32[]{:T(128)}) all-reduce(f32[]{:T(128)} %get-tuple-element.5, f32[]{:T(128)} %get-tuple-element.4), channel_id=1, replica_groups=mesh['col'=32,'leg'=4] {'col','leg'}, use_global_device_ids=true, to_apply=%region_1.0 | all-reduce | flops 2 | bytes 16 | tf_op jit(solution)/shard_map/psum | solution.py:35
  90.5 4.3 fusion.18
  94.9 8.9 fusion
  103.8 9.6 fusion.2
  113.3 9.3 copy.22
  122.8 5.9 fusion.17
  128.6 1.0 convolution_negate_fusion
  129.7 71.0 %reduce-scatter.8.cloned.1.call-done = f32[32,128,128]{1,2,0:T(8,128)} async-done(((f32[128,128,128]{1,2,0:T(8,128)}), f32[32,128,128]{1,2,0:T(8,128)}) %reduce-scatter.8.cloned.1.call-update) | async-done | bytes 2097168 | tf_op jit(solution)/shard_map/reduce_scatter | solution.py:76
  200.9 22.2 %reduce-scatter.6.cloned.1.call-done = f32[32,128]{1,0:T(8,128)} async-done(((f32[128,128]{1,0:T(8,128)}), f32[32,128]{1,0:T(8,128)}) %reduce-scatter.6.cloned.1.call-update) | async-done | bytes 16400 | tf_op jit(solution)/shard_map/reduce_scatter | solution.py:75
  223.1 126.4 %psum.72 = f32[32,128]{1,0:T(8,128)S(1)} all-reduce(f32[32,128]{1,0:T(8,128)} %reduce-scatter.6.cloned.1.call-done), channel_id=1, replica_groups=mesh['col'=32,'leg'=4] {'col'}, use_global_device_ids=true, to_apply=%region_5.0 | all-reduce | flops 4096 | bytes 32768 | tf_op jit(solution)/shard_map/psum | solution.py:73
  349.5 3.3 broadcast_add_fusion
  352.8 2.9 copy.24
  355.7 3.2 fusion.8
  358.9 375.8 %custom-call.11 = f32[32,128,128]{2,1,0:T(8,128)S(1)} custom-call(f32[32,128,128]{2,1,0:T(8,128)} %fusion.8), custom_call_target="Cholesky" | custom-call | tf_op jit(solution)/shard_map/vmap(jit(cholesky))/cholesky | solution.py:16
  735.0 1.7 select_bitcast_fusion
  736.7 315.5 %custom-call.12 = f32[32,1,128,128]{2,3,1,0:T(8,128)S(1)} custom-call(f32[32,1,128,128]{3,2,1,0:T(8,128)} %select_bitcast_fusion), custom_call_target="InvertDiagBlocksLowerTriangular" | custom-call | tf_op jit(solution)/shard_map/vmap(jit(_cho_solve))/triangular_solve | solution.py:17
  1052.2 1.3 copy-done.5
  1053.5 3.5 fusion.6
  1057.0 4.0 fusion.4
  1061.0 3.3 fusion.44
  1064.4 12.0 all_gather.34
  1076.6 2.4 fusion.15
  1079.1 3.7 fusion.14
  1082.8 1.0 fusion.25
  1083.8 15.1 %reduce-scatter.10.cloned.1.call-done = f32[32,128]{1,0:T(8,128)} async-done(((f32[128,128]{1,0:T(8,128)}), f32[32,128]{1,0:T(8,128)}) %reduce-scatter.10.cloned.1.call-update) | async-done | bytes 16400 | tf_op jit(solution)/shard_map/reduce_scatter | solution.py:93
  1099.0 24.9 %all-gather = f32[1024,128]{1,0:T(8,128)S(1)} all-gather(f32[32,128]{1,0:T(8,128)} %reduce-scatter.10.cloned.1.call-done), channel_id=2, replica_groups=mesh['col'=32,'leg'=4] {'col'}, dimensions={0}, use_global_device_ids=true | all-gather | bytes 540672 | tf_op jit(solution)/shard_map/all_gather | solution.py:99
  1124.6 9.2 all-reduce.1
  1135.1 3.3 fusion.45
  1139.0 9.5 psum.76
  1149.9 12.2 all_gather.37
  1162.4 4.2 fusion.13
  1166.6 3.7 fusion.12
  1170.3 1.0 fusion.23
  1171.3 18.1 %reduce-scatter.12.cloned.1.call-done = f32[32,128]{1,0:T(8,128)} async-done(((f32[128,128]{1,0:T(8,128)}), f32[32,128]{1,0:T(8,128)}) %reduce-scatter.12.cloned.1.call-update) | async-done | bytes 16400 | tf_op jit(solution)/shard_map/reduce_scatter | solution.py:93
  1189.4 25.0 %all-gather.1 = f32[1024,128]{1,0:T(8,128)S(1)} all-gather(f32[32,128]{1,0:T(8,128)} %reduce-scatter.12.cloned.1.call-done), channel_id=3, replica_groups=mesh['col'=32,'leg'=4] {'col'}, dimensions={0}, use_global_device_ids=true | all-gather | bytes 540672 | tf_op jit(solution)/shard_map/all_gather | solution.py:99
  1215.0 9.2 psum.77
  1225.5 3.3 fusion.46
  1229.5 9.5 psum.78
  1240.4 12.2 all_gather.40
  1252.8 4.2 fusion.11
  1257.0 3.7 fusion.10
  1261.7 18.1 %reduce-scatter.14.cloned.1.call-done = f32[32,128]{1,0:T(8,128)} async-done(((f32[128,128]{1,0:T(8,128)}), f32[32,128]{1,0:T(8,128)}) %reduce-scatter.14.cloned.1.call-update) | async-done | bytes 16400 | tf_op jit(solution)/shard_map/reduce_scatter | solution.py:93
  1279.9 24.9 %all-gather.2 = f32[1024,128]{1,0:T(8,128)S(1)} all-gather(f32[32,128]{1,0:T(8,128)} %reduce-scatter.14.cloned.1.call-done), channel_id=4, replica_groups=mesh['col'=32,'leg'=4] {'col'}, dimensions={0}, use_global_device_ids=true | all-gather | bytes 540672 | tf_op jit(solution)/shard_map/all_gather | solution.py:99
  1305.5 9.2 psum.79
  1316.0 11.9 all_gather.43
  1328.1 4.2 fusion.16
  (69 shorter events, 9.0 us)
Async XLA Ops:
  7.2 87.7 %copy-start.6 = (f32[16,128]{1,0:T(8,128)S(1)}, f32[16,128]{1,0:T(8,128)}, u32[]{:S(2)}) copy-start(f32[16,128]{1,0:T(8,128)} %param.11) | copy-start | bytes 24580
  7.2 87.7 %copy-start.7 = (f32[16,128]{1,0:T(8,128)S(1)}, f32[16,128]{1,0:T(8,128)}, u32[]{:S(2)}) copy-start(f32[16,128]{1,0:T(8,128)} %param.12) | copy-start | bytes 24580
  7.2 87.7 %copy-start.8 = (f32[16,128]{1,0:T(8,128)S(1)}, f32[16,128]{1,0:T(8,128)}, u32[]{:S(2)}) copy-start(f32[16,128]{1,0:T(8,128)} %param.13) | copy-start | bytes 24580
  7.2 193.5 %reduce-scatter.8.cloned.1.call-start = ((), (), s32[]{:S(2)}) async-start(), calls=%async_computation.6 | async-start | bytes 10485760 | tf_op jit(solution)/shard_map/reduce_scatter | solution.py:76
  90.5 4.4 copy-start
  122.7 226.8 %copy-start.9 = (f32[32,128]{1,0:T(8,128)S(1)}, f32[32,128]{1,0:T(8,128)}, u32[]{:S(2)}) copy-start(f32[32,128]{1,0:T(8,128)} %param.15) | copy-start | bytes 49156
  122.7 100.3 %reduce-scatter.6.cloned.1.call-start = ((), (), s32[]{:S(2)}) async-start(), calls=%async_computation.5 | async-start | bytes 81920 | tf_op jit(solution)/shard_map/reduce_scatter | solution.py:75
  129.6 219.9 %all-reduce.4.cloned.1.call-start = ((), (), s32[]{:S(2)}) async-start(), calls=%async_computation.7 | async-start | bytes 4194304 | tf_op jit(solution)/shard_map/psum | solution.py:73
  200.7 898.3 %reduce-scatter.10.cloned.1.call-start = ((), (), s32[]{:S(2)}) async-start(), calls=%async_computation.8 | async-start | bytes 81920 | tf_op jit(solution)/shard_map/reduce_scatter | solution.py:93
  349.5 6.2 copy-start.4
  1052.2 1.4 copy-start.5
  1057.0 19.6 %copy-start.1 = (f32[16,4,128,128]{3,2,1,0:T(8,128)S(1)}, f32[16,4,128,128]{3,2,1,0:T(8,128)}, u32[]{:S(2)}) copy-start(f32[16,4,128,128]{3,2,1,0:T(8,128)} %param.8) | copy-start | bytes 12582916
  1083.8 105.6 %reduce-scatter.12.cloned.1.call-start = ((), (), s32[]{:S(2)}) async-start(), calls=%async_computation.9 | async-start | bytes 81920 | tf_op jit(solution)/shard_map/reduce_scatter | solution.py:93
  1149.9 16.6 %copy-start.2 = (f32[16,4,128,128]{3,2,1,0:T(8,128)S(1)}, f32[16,4,128,128]{3,2,1,0:T(8,128)}, u32[]{:S(2)}) copy-start(f32[16,4,128,128]{3,2,1,0:T(8,128)} %param.8) | copy-start | bytes 12582916
  1171.3 108.6 %reduce-scatter.14.cloned.1.call-start = ((), (), s32[]{:S(2)}) async-start(), calls=%async_computation.10 | async-start | bytes 81920 | tf_op jit(solution)/shard_map/reduce_scatter | solution.py:93
  1240.3 16.7 %copy-start.3 = (f32[16,4,128,128]{3,2,1,0:T(8,128)S(1)}, f32[16,4,128,128]{3,2,1,0:T(8,128)}, u32[]{:S(2)}) copy-start(f32[16,4,128,128]{3,2,1,0:T(8,128)} %param.8) | copy-start | bytes 12582916
  1257.0 75.3 %copy-start.10 = (s32[16]{0:T(128)S(1)}, s32[16]{0:T(128)}, u32[]{:S(2)}) copy-start(s32[16]{0:T(128)} %param.10) | copy-start | bytes 196
Sparse Core Ops, SparseCore 0:
  122.8 77.7 reduce-scatter.7
  203.0 20.0 reduce-scatter.5
  226.7 107.2 all-reduce.3
  1083.9 15.0 reduce-scatter.9
  1171.4 17.9 reduce-scatter.11
  1261.9 17.9 reduce-scatter.13
